TPU v7x, 256 devices: a whole 4x4x8 slice. The times are simulated.
256 devices in a mesh: ens: 8 (over y, z_hi), tile: 32 (over z_lo, x, core).
Axes of the slice: x: 4, y: 4, z: 8 (z_hi: 2, z_lo: 4; z = z_hi * 4 + z_lo), core: 2. Of those that a mesh axis runs over, the one named last changes fastest.
Arguments:
- fields: bfloat16 [8, 32, 200, 8, 128], P('ens', 'tile'), may hold values from -6 to 6
- target: bfloat16 [8, 32, 200, 8, 128], P('ens', 'tile'), may hold values from -6 to 6
- wet_levels: int32 [32, 8, 128], P('tile'), may hold values from 0 to 19, as said below
- tile_links: int32 [32, 5], replicated, may hold values from -1 to 31, as said below
- tile_owner: int32 [32], replicated, may hold values from 0 to 31, as said below
- kernel: float32 [200, 49], replicated, may hold values from -0.875 to 0.875
- norm_gain: float32 [200], replicated, may hold values from 0.5 to 1.5
- weight_in: bfloat16 [200, 800], replicated, may hold values from -0.4375 to 0.4375
- weight_out: bfloat16 [800, 200], replicated, may hold values from -0.21875 to 0.21875
- layer_scale: float32 [200], replicated, may hold values from 0.25 to 1
Outputs:
- block_out: bfloat16 [8, 32, 200, 8, 128], P('ens', 'tile')
- grad_in: float32 [200, 800], replicated
- grad_out: float32 [800, 200], replicated
- grad_kernel: float32 [200, 49], replicated
Inputs may be any that keep to these rules, and one draw needn't show every extreme that they name: `wet_levels`: 0 is land; a cell is wet at the levels below its value. `tile_links`: the kept tiles are the kept blocks of a grid 8 tiles wide, numbered row by row from the south. West and east wrap around within a grid row; the southmost row has no south neighbour; the northmost row is complete, its north neighbour is the tile of the same row in the mirrored column 7 - column, and only it has flag 1 in column 4; -1 marks a missing neighbour. Column 4 is 0 or 1. `tile_owner`: a permutation.
All inputs are finite; a program needn't handle non-finite values.
Results may differ from a plain program's by a relative error of at most 0.005.
Values may be sent and summed in bfloat16 or wider, within the bound.
No kernel may reach another device: no remote copies, remote signals or barrier semaphores. Data moves between devices by JAX's collectives and lax.ppermute only.
A program may use at most 192 MiB of HBM per device.

v0:
```python
import jax
import jax.numpy as jnp
from jax import lax
from jax.sharding import PartitionSpec as P

LEVELS = 19
root_half = 0.7071067811865476
gauss_norm = 0.3989422804014327
norm_epsilon = 1e-06


def gelu_value(values):
    return 0.5 * values * (1.0 + lax.erf(values * root_half))


def gelu_slope(values):
    return (
        0.5 * (1.0 + lax.erf(values * root_half))
        + values * jnp.exp(-0.5 * values * values) * gauss_norm
    )


def take_slot(held, pieces, slot_id):
    piece_count = pieces.shape[0]
    inside = (slot_id >= 0) & (slot_id >= 0) & (slot_id < piece_count)
    taken = lax.dynamic_index_in_dim(
        pieces, jnp.clip(slot_id, 0, piece_count - 1), 0, keepdims=False
    )
    return jnp.where(inside, taken, held)


def local(
    fields,
    target,
    wet_levels,
    tile_links,
    tile_owner,
    kernel,
    norm_gain,
    weight_in,
    weight_out,
    layer_scale,
):
    members, _, channels, row_count, col_count = fields.shape
    tile_count = tile_owner.shape[0]
    own_slot = lax.axis_index("tile")
    own_tile = jnp.sum(
        jnp.where(tile_owner == own_slot, jnp.arange(tile_count, dtype=jnp.int32), 0)
    )
    level_of = jnp.arange(channels, dtype=jnp.int32) * LEVELS // channels
    wet_mask = wet_levels[0][None, :, :] > level_of[:, None, None]
    own_input = fields[:, 0]
    masked = jnp.where(wet_mask[None], own_input, jnp.zeros_like(own_input))
    entry_total = jnp.float32(
        members * lax.axis_size("ens") * tile_count * channels * row_count * col_count
    )

    def link_of(tile_id, column):
        return jnp.where(tile_id >= 0, tile_links[jnp.clip(tile_id, 0, tile_count - 1), column], -1)

    def slot_of(tile_id):
        return jnp.where(tile_id >= 0, tile_owner[jnp.clip(tile_id, 0, tile_count - 1)], -1)

    north_slot = slot_of(link_of(own_tile, 0))
    south_slot = slot_of(link_of(own_tile, 1))
    own_fold = link_of(own_tile, 4)
    west_tile = link_of(own_tile, 2)
    east_tile = link_of(own_tile, 3)
    west_slot = slot_of(west_tile)
    east_slot = slot_of(east_tile)
    zero_rows = jnp.zeros((members, channels, 3, col_count), jnp.bfloat16)
    row_strips = jnp.stack([masked[:, :, :3, :], masked[:, :, row_count - 3 :, :]], axis=0)[None]
    held = (zero_rows, zero_rows, zero_rows)
    pieces = lax.all_gather(row_strips, "tile", axis=0, tiled=True)
    lower_rows = take_slot(held[0], pieces[:, 0], north_slot)
    upper_rows = take_slot(held[1], pieces[:, 1], north_slot)
    below_rows = take_slot(held[2], pieces[:, 1], south_slot)
    north_rows = jnp.where(own_fold == 1, jnp.flip(upper_rows, (2, 3)), lower_rows)
    center = jnp.concatenate([below_rows, masked, north_rows], axis=2)
    side_cols = jnp.swapaxes(
        jnp.stack([center[..., :3], center[..., col_count - 3 :]], axis=0), 3, 4
    )[None]
    zero_cols = jnp.zeros((members, channels, 3, row_count + 6), jnp.bfloat16)
    held = (zero_cols, zero_cols)
    pieces = lax.all_gather(side_cols, "tile", axis=0, tiled=True)
    west_part = take_slot(held[0], pieces[:, 1], west_slot)
    east_part = take_slot(held[1], pieces[:, 0], east_slot)
    west_cols = jnp.swapaxes(west_part, 2, 3)
    east_cols = jnp.swapaxes(east_part, 2, 3)
    extended = jnp.concatenate([west_cols, center, east_cols], axis=3).astype(jnp.float32)
    conv_out = jnp.zeros((members, channels, row_count, col_count), jnp.float32)
    for row_off in range(7):
        for col_off in range(7):
            conv_out = (
                conv_out
                + kernel[:, 7 * row_off + col_off][None, :, None, None]
                * extended[:, :, row_off : row_off + row_count, col_off : col_off + col_count]
            )
    chan_mean = jnp.mean(conv_out, axis=1, keepdims=True)
    chan_var = jnp.mean((conv_out - chan_mean) ** 2, axis=1, keepdims=True)
    inv_std = 1.0 / jnp.sqrt(chan_var + norm_epsilon)
    centred = (conv_out - chan_mean) * inv_std
    gain_wide = norm_gain[None, :, None, None]
    scale_wide = layer_scale[None, :, None, None]
    normed = (centred * gain_wide).astype(jnp.bfloat16)
    flat_norm = normed.reshape(members, channels, row_count * col_count)
    hidden = jnp.einsum("ch,ecp->ehp", weight_in, flat_norm, preferred_element_type=jnp.float32)
    activated = gelu_value(hidden).astype(jnp.bfloat16)
    mlp_out = jnp.einsum("hc,ehp->ecp", weight_out, activated, preferred_element_type=jnp.float32)
    mlp_out = mlp_out.reshape(members, channels, row_count, col_count)
    block_out = (masked.astype(jnp.float32) + scale_wide * mlp_out).astype(jnp.bfloat16)
    misfit = jnp.where(
        wet_mask[None], block_out.astype(jnp.float32) - target[:, 0].astype(jnp.float32), 0.0
    )
    grad_mlp = (
        (2.0 * scale_wide * misfit)
        .astype(jnp.bfloat16)
        .reshape(members, channels, row_count * col_count)
    )
    part_out = jnp.einsum("ehp,ecp->hc", activated, grad_mlp, preferred_element_type=jnp.float32)
    grad_act = jnp.einsum("hc,ecp->ehp", weight_out, grad_mlp, preferred_element_type=jnp.float32)
    grad_hidden = (grad_act * gelu_slope(hidden)).astype(jnp.bfloat16)
    part_in = jnp.einsum("ecp,ehp->ch", flat_norm, grad_hidden, preferred_element_type=jnp.float32)
    grad_normed = jnp.einsum(
        "ch,ehp->ecp", weight_in, grad_hidden, preferred_element_type=jnp.float32
    )
    grad_scaled = grad_normed.reshape(members, channels, row_count, col_count) * gain_wide
    grad_conv = (
        grad_scaled
        - jnp.mean(grad_scaled, axis=1, keepdims=True)
        - centred * jnp.mean(grad_scaled * centred, axis=1, keepdims=True)
    ) * inv_std
    kernel_terms = []
    for row_off in range(7):
        for col_off in range(7):
            kernel_terms.append(
                jnp.sum(
                    grad_conv
                    * extended[:, :, row_off : row_off + row_count, col_off : col_off + col_count],
                    axis=(0, 2, 3),
                )
            )
    part_kernel = jnp.stack(kernel_terms, axis=1)
    sum_in, sum_out, sum_kernel = lax.psum((part_in, part_out, part_kernel), ("ens", "tile"))
    return (
        block_out[:, None],
        sum_in / entry_total,
        sum_out / entry_total,
        sum_kernel / entry_total,
    )


def solution(mesh):
    placed = (
        P("ens", "tile", None, None, None),
        P("ens", "tile", None, None, None),
        P("tile", None, None),
        P(),
        P(),
        P(),
        P(),
        P(),
        P(),
        P(),
    )
    return jax.shard_map(
        local,
        mesh=mesh,
        in_specs=placed,
        out_specs=(P("ens", "tile", None, None, None), P(), P(), P()),
        check_vma=False,
    )
```

profile of v0, /device:TPU:8, one launch (start us, length us, event | category | flops | bytes accessed | tf_op | source)
XLA Modules:
  0.0 526.0 jit_solution(14262006590394135632)
XLA Ops:
  7.2 0.0 copy-start
  7.2 0.0 all-gather.5.cloned.1.call-start
  7.2 1.2 compare_select_fusion.2
  8.5 0.0 copy-start.3
  8.5 0.8 pad_maximum_fusion.1
  9.3 0.0 all-gather.5.cloned.1.call-update
  9.3 0.0 all-gather.7.cloned.1.call-start
  9.4 1.3 fusion.30
  12.0 1.5 constant_dynamic-slice_fusion.3
  16.0 1.5 fusion.43
  19.4 65.3 %all-gather.5.cloned.1.call-done = bf16[64,1,200,3,128]{4,2,3,1,0:T(8,128)(2,1)} async-done(((bf16[2,1,200,3,128]{4,2,3,1,0:T(8,128)(2,1)}), bf16[64,1,200,3,128]{4,2,3,1,0:T(8,128)(2,1)}) %all-gather.5.cloned.1.call-update) | async-done | bytes 9830416 | tf_op jit(solution)/shard_map/all_gather | solution.py:74
  84.7 9.3 %fusion.39 = (bf16[32,1,1,200,3,128]{5,3,4,2,1,0:T(8,128)(2,1)}, bf16[32,1,1,200,3,128]{5,3,4,2,1,0:T(8,128)(2,1)}) fusion(bf16[32,2,1,200,3,128]{5,3,4,2,1,0:T(8,128)(2,1)} %bitcast.230), kind=kLoop, calls=%fused_computation.131 | loop fusion | bytes 19660800 | tf_op jit(solution)/shard_map/slice | solution.py:75
  94.1 1.0 select_bitcast_fusion.3
  95.1 0.9 rev.4
  96.1 1.0 bitcast_select_fusion
  97.0 0.1 pad_maximum_fusion
  97.1 0.0 copy-start.4
  97.2 0.3 slice_bitcast_fusion.1
  97.4 0.0 copy-start.9
  97.4 0.0 copy-start.12
  97.5 0.3 maximum_bitcast_fusion
  97.8 1.3 copy.28
  99.1 0.0 all-gather.7.cloned.1.call-update
  99.2 0.2 all-reduce.3.cloned.1.call-start
  100.7 0.9 squeeze.55
  101.6 1.1 reshape.540
  102.7 0.6 broadcast_multiply_fusion.5
  103.3 0.6 fusion.42
  103.9 0.7 fusion.40
  104.6 0.7 fusion.41
  105.3 52.3 %all-gather.7.cloned.1.call-done = bf16[64,1,200,3,14]{2,4,3,1,0:T(8,128)(2,1)} async-done(((bf16[2,1,200,3,14]{2,4,3,1,0:T(8,128)(2,1)}), bf16[64,1,200,3,14]{2,4,3,1,0:T(8,128)(2,1)}) %all-gather.7.cloned.1.call-update) | async-done | bytes 1075216 | tf_op jit(solution)/shard_map/all_gather | solution.py:85
  157.6 28.8 %copy.29 = bf16[64,1,200,3,14]{3,2,4,0,1:T(8,128)(2,1)} copy(bf16[64,1,200,3,14]{2,4,3,1,0:T(8,128)(2,1)} %all-gather.7.cloned.1.call-done) | data formatting | bytes 2150400 | tf_op jit(solution)/shard_map/all_gather | solution.py:85
  186.4 30.0 %fusion.38 = (bf16[32,1,1,200,3,14]{4,3,5,2,1,0:T(8,128)(2,1)}, bf16[32,1,1,200,3,14]{4,3,5,2,1,0:T(8,128)(2,1)}) fusion(bf16[32,2,1,200,3,14]{4,3,5,2,1,0:T(8,128)(2,1)} %bitcast.229), kind=kLoop, calls=%fused_computation.130 | loop fusion | bytes 2150400 | tf_op jit(solution)/shard_map/slice | solution.py:86
  216.3 1.4 select_bitcast_fusion
  217.8 0.0 copy-start.14
  218.1 1.8 maximum_convert_fusion
  220.3 11.7 %fusion.37 = (f32[8,128]{1,0:T(8,128)S(1)}, f32[1,200,8,128]{3,1,2,0:T(8,128)S(1)}) fusion(f32[1,200,14,134]{3,1,2,0:T(8,128)S(1)} %maximum_convert_fusion, f32[200]{0:T(256)S(1)} %bitcast.247, f32[200]{0:T(256)S(1)} %bitcast.248, f32[200]{0:T(256)S(1)} %bitcast.250, f32[200]{0:T(256)S(1)} %bitcast.251, f32[200]{0:T(256)S(1)} %bitcast.252, ...), kind=kLoop, calls=%fused_computation.129 | loop fusion | flops 20069376 | bytes 41003296 | tf_op jit(solution)/shard_map/reduce_sum | solution.py:99
  232.1 0.0 copy-start.53
  232.1 0.1 multiply_reduce_fusion.50
  232.2 0.1 multiply_convert_fusion
  232.4 0.1 copy.30
  232.4 0.6 fusion.22
  233.1 0.3 copy-done.53
  233.4 1.5 fusion.28
  234.9 0.9 copy-done.6
  235.8 0.3 fusion.20
  236.1 1.7 fusion.5
  237.8 1.8 fusion.26
  239.6 1.5 fusion.17
  241.1 1.6 fusion.13
  242.7 1.6 multiply_reduce_fusion.49
  244.3 6.1 %multiply_reduce_fusion = (f32[200]{0:T(256)S(1)}, f32[200]{0:T(256)S(1)}, f32[200]{0:T(256)S(1)}, f32[200]{0:T(256)S(1)}, f32[200]{0:T(256)S(1)}, /*index=5*/f3...) fusion(f32[1,200,14,134]{3,1,2,0:T(8,128)S(1)} %maximum_convert, ...), kind=kLoop, calls=%fused_computation.30 | loop fusion | flops 8802800 | bytes 17234784 | tf_op jit(solution)/shard_map/reduce_sum | solution.py:137
  250.4 0.9 copy-done.2
  251.3 4.7 multiply_reduce_fusion.18
  256.0 0.0 all-reduce.3.cloned.1.call-update
  256.1 4.6 multiply_reduce_fusion.36
  260.7 0.2 copy.34
  260.8 0.2 stack.223
  261.0 76.9 %psum.23 = f32[200,49]{0,1:T(8,128)S(1)} all-reduce(f32[200,49]{0,1:T(8,128)S(1)} %stack.223), channel_id=1, replica_groups=mesh['ens'=8,'tile'=32] {'ens','tile'}, use_global_device_ids=true, to_apply=%region_56.57 | all-reduce | flops 9800 | bytes 78400 | tf_op jit(solution)/shard_map/psum | solution.py:144
  337.9 0.6 broadcast_multiply_fusion.2
  338.5 2.4 add_convert_fusion
  340.9 174.4 %all-reduce.3.cloned.1.call-done = (f32[200,800]{1,0:T(8,128)}, f32[800,200]{0,1:T(8,128)}) async-done(((f32[200,800]{1,0:T(8,128)}, f32[800,200]{0,1:T(8,128)}), (f32[200,800]{1,0:T(8,128)}, f32[800,200]{0,1:T(8,128)})) %all-reduce.3.cloned.1.call-update) | async-done | bytes 1280016 | tf_op jit(solution)/shard_map/psum | solution.py:144
  515.4 2.0 broadcast_multiply_fusion
  517.4 2.0 broadcast_multiply_fusion.1
  (104 shorter events, 0.3 us)
Async XLA Ops:
  7.2 225.3 %copy-start = (bf16[200,800]{1,0:T(8,128)(2,1)S(1)}, bf16[200,800]{1,0:T(8,128)(2,1)}, u32[]{:S(2)}) copy-start(bf16[200,800]{1,0:T(8,128)(2,1)} %param.17) | copy-start | bytes 960004
  7.2 77.5 %all-gather.5.cloned.1.call-start = ((), (), s32[]{:S(2)}) async-start(), calls=%async_computation | async-start | bytes 10137600 | tf_op jit(solution)/shard_map/all_gather | solution.py:74
  8.5 88.6 %copy-start.3 = (bf16[1,200,8,128]{3,1,2,0:T(8,128)(2,1)}, bf16[1,200,8,128]{3,1,2,0:T(8,128)(2,1)S(1)}, u32[]{:S(2)}) copy-start(bf16[1,200,8,128]{3,1,2,0:T(8,128)(2,1)S(1)} %compare_select_fusion.2) | copy-start | bytes 1228804
  9.3 148.2 %all-gather.7.cloned.1.call-start = ((), (), s32[]{:S(2)}) async-start(), calls=%async_computation.1 | async-start | bytes 1622016 | tf_op jit(solution)/shard_map/all_gather | solution.py:85
  97.1 3.5 copy-start.4
  97.4 4.2 copy-start.9
  97.4 5.3 %copy-start.12 = (f32[200]{0:T(256)S(1)}, f32[200]{0:T(256)}, u32[]{:S(2)}) copy-start(f32[200]{0:T(256)} %param.19) | copy-start | bytes 2404
  97.5 5.8 %copy-start.10 = (f32[200,49]{0,1:T(8,128)S(1)}, f32[200,49]{0,1:T(8,128)}, u32[]{:S(2)}) copy-start(f32[200,49]{0,1:T(8,128)} %param.15) | copy-start | bytes 117604
  99.2 416.2 %all-reduce.3.cloned.1.call-start = ((), (), s32[]{:S(2)}) async-start(), calls=%async_computation.2 | async-start | bytes 2867200 | tf_op jit(solution)/shard_map/psum | solution.py:144
  217.8 2.2 copy-start.14
  217.8 2.2 copy-start.15
  217.8 2.2 copy-start.16
  217.8 2.2 copy-start.17
  217.8 2.2 copy-start.18
  217.8 2.2 copy-start.19
  217.8 2.2 copy-start.20
  217.8 2.2 copy-start.21
  217.8 2.2 copy-start.22
  217.9 2.2 copy-start.23
  217.9 2.2 copy-start.24
  217.9 2.2 copy-start.25
  217.9 2.2 copy-start.26
  217.9 2.2 copy-start.27
  217.9 2.2 copy-start.28
  217.9 2.2 copy-start.29
  217.9 2.2 copy-start.30
  217.9 2.2 copy-start.31
  217.9 2.2 copy-start.32
  218.0 2.2 copy-start.33
  218.0 2.2 copy-start.34
  218.0 2.2 copy-start.35
  218.0 2.2 copy-start.36
  218.0 2.2 copy-start.37
  218.0 2.2 copy-start.38
  218.0 2.2 copy-start.39
  218.0 2.2 copy-start.40
  218.0 2.2 copy-start.41
  218.0 2.2 copy-start.42
  218.1 2.2 copy-start.43
  218.1 2.2 copy-start.44
  218.1 2.2 copy-start.45
  218.1 2.2 copy-start.46
  218.1 2.2 copy-start.47
  218.1 2.2 copy-start.48
  218.1 2.2 copy-start.49
  218.1 2.2 copy-start.50
  218.1 2.2 copy-start.51
  220.3 11.9 %copy-start.13 = (f32[200]{0:T(256)S(1)}, f32[200]{0:T(256)}, u32[]{:S(2)}) copy-start(f32[200]{0:T(256)} %param.16) | copy-start | bytes 2404
  232.1 1.0 copy-start.1
  232.1 1.3 copy-start.53
  233.3 2.4 copy-start.5
  233.4 2.4 copy-start.8
  233.4 2.4 copy-start.11
  233.4 2.4 copy-start.52
  234.9 0.9 copy-start.6
  250.4 0.9 copy-start.2
  256.1 4.6 copy-start.7
Sparse Core Ops, SparseCore 0:
  10.4 74.2 all-gather.4
  99.3 58.2 all-gather.6
  256.2 259.1 all-reduce.2
where the time goes:
time: 528 us; the launch traced here: 526 us
  waiting for transfers between devices  292 us (55%)
  local copies, waits for them, and re-layouts  80.3 us (15%)
  blocking collectives  76.9 us (15%)
  other arithmetic  45.9 us (9%)
  between operations  21.6 us (4%)
  matrix products  8.73 us (2%)
    psum x1, waiting for transfers between devices, local(): lax.psum((part_in, part_out, part_kernel), ('ens', 'tile'))  174 us
    psum x1, blocking collectives, local(): lax.psum((part_in, part_out, part_kernel), ('ens', 'tile'))  76.9 us
    all_gather x1, waiting for transfers between devices, local(): pieces = lax.all_gather(row_strips, 'tile', axis=0, tiled=True)  65.3 us
    all_gather x1, waiting for transfers between devices, local(): pieces = lax.all_gather(side_cols, 'tile', axis=0, tiled=True)  52.3 us
    slice x1, local copies, waits for them, and re-layouts, local(): west_part = take_slot(held[0], pieces[:, 1], west_slot)  30 us
    all_gather x1, local copies, waits for them, and re-layouts, local(): pieces = lax.all_gather(side_cols, 'tile', axis=0, tiled=True)  28.8 us
    reduce_sum x3, other arithmetic, local(): jnp.sum(grad_conv * extended[:, :, row_off:row_off + row_count, col_off:c...  15.4 us
    reduce_sum x1, other arithmetic, local(): chan_mean = jnp.mean(conv_out, axis=1, keepdims=True)  11.7 us
  transfers between devices with their start and end apart: 3, of which 3 were waited for; matrix products, arithmetic and copies ran while one was open for 3% of the time, Pallas kernels for 0%

commit v1 on v0

--- a/solution.py
+++ b/solution.py
@@ -71,7 +71,9 @@
     zero_rows = jnp.zeros((members, channels, 3, col_count), jnp.bfloat16)
     row_strips = jnp.stack([masked[:, :, :3, :], masked[:, :, row_count - 3 :, :]], axis=0)[None]
     held = (zero_rows, zero_rows, zero_rows)
-    pieces = lax.all_gather(row_strips, "tile", axis=0, tiled=True)
+    pieces = jnp.concatenate(
+        lax.all_to_all(jnp.stack([row_strips] * lax.axis_size("tile")), "tile", 0, 0), axis=0
+    )
     lower_rows = take_slot(held[0], pieces[:, 0], north_slot)
     upper_rows = take_slot(held[1], pieces[:, 1], north_slot)
     below_rows = take_slot(held[2], pieces[:, 1], south_slot)

time: 528 us -> 658 us (1.25)
  waiting for transfers between devices: 292 us -> 443 us
  local copies, waits for them, and re-layouts: 80.3 us -> 61.6 us
  other arithmetic: 45.9 us -> 35.1 us
  starting transfers between devices: 0.3 us -> 9.08 us
    all_to_all x0 -> x1, waiting for transfers between devices: none -> 210 us  [local(): lax.all_to_all(jnp.stack([row_strips] * lax.axis_size('tile')), 'tile', 0...]
    all_gather x1 -> x0, waiting for transfers between devices: 65.3 us -> none  [local(): pieces = lax.all_gather(row_strips, 'tile', axis=0, tiled=True)]
    all_gather x1 -> x0, local copies, waits for them, and re-layouts: 28.8 us -> none  [local(): pieces = lax.all_gather(side_cols, 'tile', axis=0, tiled=True)]
    slice x1, local copies, waits for them, and re-layouts: 30 us -> 1.48 us  [local(): west_part = take_slot(held[0], pieces[:, 1], west_slot)]
    all_to_all x0 -> x1, local copies, waits for them, and re-layouts: none -> 24.6 us  [local(): lax.all_to_all(jnp.stack([row_strips] * lax.axis_size('tile')), 'tile', 0...]
    all_to_all x0 -> x1, starting transfers between devices: none -> 9 us  [local(): lax.all_to_all(jnp.stack([row_strips] * lax.axis_size('tile')), 'tile', 0...]
  transfers between devices with their start and end apart: 3 -> 3, of which waited for: 3 -> 3; matrix products, arithmetic and copies ran while one was open for 3% -> 2% of each run, Pallas kernels for 0% -> 0%
where the time goes in v1:
time: 658 us; the launch traced here: 656 us
  waiting for transfers between devices  443 us (67%)
  blocking collectives  76.6 us (12%)
  local copies, waits for them, and re-layouts  61.6 us (9%)
  other arithmetic  35.1 us (5%)
  between operations  22.1 us (3%)
  matrix products  9.25 us (1%)
  starting transfers between devices  9.08 us (1%)
    all_to_all x1, waiting for transfers between devices, local(): lax.all_to_all(jnp.stack([row_strips] * lax.axis_size('tile')), 'tile', 0...  210 us
    psum x1, waiting for transfers between devices, local(): lax.psum((part_in, part_out, part_kernel), ('ens', 'tile'))  177 us
    psum x1, blocking collectives, local(): lax.psum((part_in, part_out, part_kernel), ('ens', 'tile'))  76.6 us
    all_gather x1, waiting for transfers between devices, local(): pieces = lax.all_gather(side_cols, 'tile', axis=0, tiled=True)  55.1 us
    all_to_all x1, local copies, waits for them, and re-layouts, local(): lax.all_to_all(jnp.stack([row_strips] * lax.axis_size('tile')), 'tile', 0...  24.6 us
  transfers between devices with their start and end apart: 3, of which 3 were waited for; matrix products, arithmetic and copies ran while one was open for 2% of the time, Pallas kernels for 0%

profile of v1, /device:TPU:8, one launch (start us, length us, event | category | flops | bytes accessed | tf_op | source)
XLA Modules:
  0.0 656.1 jit_solution(14268149734547880217)
XLA Ops:
  7.2 0.0 copy-start
  7.2 1.6 copy.45
  8.8 0.8 copy.44
  9.6 0.2 compare_select_fusion
  9.8 0.2 slice_bitcast_fusion.1
  10.0 0.4 maximum_bitcast_fusion
  10.4 0.3 copy.46
  10.7 5.1 stack.177
  15.8 9.0 %all-to-all-start = ((bf16[32,1,2,1,200,3,128]{6,4,5,3,2,1,0:T(8,128)(2,1)}), bf16[32,1,2,1,200,3,128]{6,4,5,3,2,1,0:T(8,128)(2,1)}, u32[]{:S(2)}, u32[]{:S(2)}) async-start(bf16[32,1,2,1,200,3,128]{6,4,5,3,2,1,0:T(8,128)(2,1)} %stack.177), calls=%async_computation | async-start | bytes 19660800 | tf_op jit(solution)/shard_map/all_to_all | solution.py:75
  24.8 0.0 all-gather.3.cloned.1.call-start
  24.9 0.6 fusion.31
  26.8 0.6 constant_dynamic-slice_fusion.3
  30.0 0.7 fusion.44
  32.6 210.3 %all-to-all-done = bf16[32,1,2,1,200,3,128]{6,4,5,3,2,1,0:T(8,128)(2,1)} async-done(((bf16[32,1,2,1,200,3,128]{6,4,5,3,2,1,0:T(8,128)(2,1)}), bf16[32,1,2,1,200,3,128]{6,4,5,3,2,1,0:T(8,128)(2,1)}, u32[]{:S(2)}, u32[]{:S(2)}) %all-to-all-start) | async-done | bytes 9830432 | tf_op jit(solution)/shard_map/all_to_all | solution.py:75
  242.9 24.6 %copy.47 = bf16[32,1,2,1,200,3,128]{4,5,6,2,0,3,1:T(4,128)(2,1)} copy(bf16[32,1,2,1,200,3,128]{6,4,5,3,2,1,0:T(8,128)(2,1)} %all-to-all-done) | data formatting | bytes 19660800 | tf_op jit(solution)/shard_map/all_to_all | solution.py:75
  267.5 13.1 %fusion.39 = (bf16[32,1,1,200,3,128]{3,4,5,2,1,0:T(4,128)(2,1)}, bf16[32,1,1,200,3,128]{3,4,5,2,1,0:T(4,128)(2,1)S(1)}) fusion(bf16[32,2,1,200,3,128]{3,4,5,2,1,0:T(4,128)(2,1)} %bitcast.223), kind=kLoop, calls=%fused_computation.130 | loop fusion | bytes 19660800 | tf_op jit(solution)/shard_map/slice | solution.py:77
  280.6 0.2 select_bitcast_fusion.1
  280.8 0.0 copy-start.9
  280.8 0.6 rev.4
  281.4 1.1 bitcast_select_fusion
  282.5 0.0 copy-start.7
  282.6 0.7 copy-done.7
  283.3 0.6 maximum_bitcast_fusion.1
  283.9 0.0 all-gather.3.cloned.1.call-update
  283.9 0.0 all-reduce.3.cloned.1.call-start
  285.3 0.9 squeeze.55
  286.2 1.1 reshape.547
  287.3 0.6 broadcast_multiply_fusion.5
  287.9 0.7 fusion.41
  288.5 0.7 fusion.42
  289.2 55.1 %all-gather.3.cloned.1.call-done = bf16[64,1,200,3,14]{2,4,3,1,0:T(8,128)(2,1)} async-done(((bf16[2,1,200,3,14]{2,4,3,1,0:T(8,128)(2,1)}), bf16[64,1,200,3,14]{2,4,3,1,0:T(8,128)(2,1)}) %all-gather.3.cloned.1.call-update) | async-done | bytes 1075216 | tf_op jit(solution)/shard_map/all_gather | solution.py:87
  344.5 1.5 fusion.40
  346.1 1.5 maximum_convert_fusion
  347.9 8.8 %fusion.38 = (f32[8,128]{0,1:T(8,128)S(1)}, f32[1,200,8,128]{1,2,3,0:T(8,128)S(1)}) fusion(f32[1,200,14,134]{1,2,3,0:T(8,128)S(1)} %maximum_convert_fusion, f32[200]{0:T(256)S(1)} %bitcast.243, f32[200]{0:T(256)S(1)} %bitcast.244, f32[200]{0:T(256)S(1)} %bitcast.246, f32[200]{0:T(256)S(1)} %bitcast.247, f32[200]{0:T(256)S(1)} %bitcast.248, ...), kind=kLoop, calls=%fused_computation.129 | loop fusion | flops 20069376 | bytes 41003296 | tf_op jit(solution)/shard_map/reduce_sum | solution.py:101
  356.8 0.4 multiply_reduce_fusion.50
  357.2 0.5 copy-done.1
  357.7 1.2 multiply_convert_fusion
  358.9 1.6 copy.48
  360.5 0.6 fusion.22
  361.2 0.3 copy-done.56
  361.5 1.5 fusion.28
  363.0 0.9 copy-done.5
  364.0 0.3 fusion.20
  364.3 1.7 fusion.5
  366.0 1.8 fusion.26
  367.8 1.6 fusion.13
  369.4 2.0 fusion.17
  371.4 1.0 copy.53
  372.5 2.6 copy.49
  375.0 2.0 multiply_reduce_fusion.49
  377.1 0.1 copy.50
  377.2 4.6 multiply_reduce_fusion
  381.8 1.0 copy-done.2
  382.8 3.1 multiply_reduce_fusion.18
  385.9 0.0 all-reduce.3.cloned.1.call-update
  385.9 3.1 multiply_reduce_fusion.36
  389.1 0.2 copy.52
  389.2 0.2 stack.230
  389.4 76.6 %psum.23 = f32[200,49]{0,1:T(8,128)S(1)} all-reduce(f32[200,49]{0,1:T(8,128)S(1)} %stack.230), channel_id=1, replica_groups=mesh['ens'=8,'tile'=32] {'ens','tile'}, use_global_device_ids=true, to_apply=%region_56.57 | all-reduce | flops 9800 | bytes 78400 | tf_op jit(solution)/shard_map/psum | solution.py:146
  466.0 0.6 broadcast_multiply_fusion.4
  466.6 1.5 add_convert_fusion
  468.1 177.1 %all-reduce.3.cloned.1.call-done = (f32[200,800]{1,0:T(8,128)}, f32[800,200]{0,1:T(8,128)}) async-done(((f32[200,800]{1,0:T(8,128)}, f32[800,200]{0,1:T(8,128)}), (f32[200,800]{1,0:T(8,128)}, f32[800,200]{0,1:T(8,128)})) %all-reduce.3.cloned.1.call-update) | async-done | bytes 1280016 | tf_op jit(solution)/shard_map/psum | solution.py:146
  645.2 2.0 broadcast_multiply_fusion.1
  647.2 2.0 broadcast_multiply_fusion
  (114 shorter events, 0.3 us)
Async XLA Ops:
  7.2 353.3 %copy-start = (bf16[200,800]{1,0:T(8,128)(2,1)S(1)}, bf16[200,800]{1,0:T(8,128)(2,1)}, u32[]{:S(2)}) copy-start(bf16[200,800]{1,0:T(8,128)(2,1)} %param.17) | copy-start | bytes 960004
  7.2 2.4 copy-start.16
  15.8 9.1 %copy-start.20 = (s32[32]{0:T(128)S(1)}, s32[32]{0:T(128)}, u32[]{:S(2)}) copy-start(s32[32]{0:T(128)} %param.14) | copy-start | bytes 388
  15.8 11.0 %copy-start.55 = (s32[32,5]{0,1:T(8,128)S(1)}, s32[32,5]{0,1:T(8,128)}, u32[]{:S(2)}) copy-start(s32[32,5]{0,1:T(8,128)} %param.13) | copy-start | bytes 1924
  15.8 227.1 %all-to-all-start = ((bf16[32,1,2,1,200,3,128]{6,4,5,3,2,1,0:T(8,128)(2,1)}), bf16[32,1,2,1,200,3,128]{6,4,5,3,2,1,0:T(8,128)(2,1)}, u32[]{:S(2)}, u32[]{:S(2)}) async-start(bf16[32,1,2,1,200,3,128]{6,4,5,3,2,1,0:T(8,128)(2,1)} %stack.177), calls=%async_computation | async-start | bytes 19660800 | tf_op jit(solution)/shard_map/all_to_all | solution.py:75
  24.8 319.4 %all-gather.3.cloned.1.call-start = ((), (), s32[]{:S(2)}) async-start(), calls=%async_computation.1 | async-start | bytes 1622016 | tf_op jit(solution)/shard_map/all_gather | solution.py:87
  280.6 4.7 copy-start.3
  280.6 5.6 copy-start.12
  280.6 6.7 %copy-start.18 = (f32[200]{0:T(256)S(1)}, f32[200]{0:T(256)}, u32[]{:S(2)}) copy-start(f32[200]{0:T(256)} %param.19) | copy-start | bytes 2404
  280.6 7.3 %copy-start.13 = (f32[200,49]{0,1:T(8,128)S(1)}, f32[200,49]{0,1:T(8,128)}, u32[]{:S(2)}) copy-start(f32[200,49]{0,1:T(8,128)} %param.15) | copy-start | bytes 117604
  280.8 65.2 %copy-start.9 = (bf16[1,200,3,128]{1,2,3,0:T(4,128)(2,1)}, bf16[1,200,3,128]{1,2,3,0:T(4,128)(2,1)S(1)}, u32[]{:S(2)}) copy-start(bf16[1,200,3,128]{1,2,3,0:T(4,128)(2,1)S(1)} %get-tuple-element.60) | copy-start | bytes 460804
  282.5 0.7 copy-start.7
  283.9 361.3 %all-reduce.3.cloned.1.call-start = ((), (), s32[]{:S(2)}) async-start(), calls=%async_computation.2 | async-start | bytes 2867200 | tf_op jit(solution)/shard_map/psum | solution.py:146
  344.2 1.8 copy-start.8
  344.2 3.4 copy-start.21
  344.2 3.4 copy-start.22
  344.2 3.4 copy-start.23
  344.2 3.4 copy-start.24
  344.3 3.4 copy-start.25
  344.3 3.4 copy-start.26
  344.3 3.4 copy-start.27
  344.3 3.4 copy-start.28
  344.3 3.4 copy-start.29
  344.3 3.4 copy-start.30
  344.3 3.4 copy-start.31
  344.3 3.4 copy-start.32
  344.3 3.4 copy-start.33
  344.3 3.4 copy-start.34
  344.4 3.4 copy-start.35
  344.4 3.4 copy-start.36
  344.4 3.4 copy-start.37
  344.4 3.4 copy-start.38
  344.4 3.4 copy-start.39
  344.4 3.4 copy-start.40
  344.4 3.4 copy-start.41
  344.4 3.4 copy-start.42
  344.4 3.4 copy-start.43
  344.4 3.4 copy-start.44
  344.5 3.4 copy-start.45
  344.5 3.4 copy-start.46
  344.5 3.4 copy-start.47
  344.5 3.4 copy-start.48
  344.5 3.4 copy-start.49
  344.5 3.4 copy-start.50
  344.5 3.4 copy-start.51
  344.5 3.4 copy-start.52
  344.5 3.4 copy-start.53
  347.9 9.8 %copy-start.15 = (f32[200]{0:T(256)S(1)}, f32[200]{0:T(256)}, u32[]{:S(2)}) copy-start(f32[200]{0:T(256)} %param.16) | copy-start | bytes 2404
  356.8 1.0 copy-start.1
  360.5 1.0 copy-start.56
  361.5 2.5 copy-start.4
  361.5 2.5 copy-start.11
  361.5 2.5 copy-start.14
  361.5 2.5 copy-start.17
  361.5 2.5 copy-start.19
  361.5 2.5 copy-start.54
  363.0 0.9 copy-start.5
  366.0 1.8 copy-start.10
  381.8 1.0 copy-start.2
  385.9 3.1 copy-start.6
Sparse Core Ops, SparseCore 0:
  284.1 60.1 all-gather.2
  386.1 259.1 all-reduce.2
